TPU v7x, 32 devices: a whole 2x2x4 slice. The times are simulated.
32 devices in a mesh: batch: 4 (over y, x), proto: 8 (over z, core).
Axes of the slice: x: 2, y: 2, z: 4, core: 2. Of those that a mesh axis runs over, the one named last changes fastest.
Arguments:
- teacher_emb: bfloat16 [256, 2048], P('proto', 'batch'), may hold values from -22 to 22
- student_emb: bfloat16 [256, 2048], P('proto', 'batch'), may hold values from -6 to 6
- prototypes: bfloat16 [256, 65536], P('batch', 'proto'), may hold values from -16 to 16
Outputs:
- grad_proto: float32 [256, 65536], P('batch', 'proto')
- grad_student: float32 [256, 2048], P('proto', 'batch')
- loss: float32 [], replicated
All inputs are finite; a program needn't handle non-finite values.
Results may differ from a plain program's by a relative error of at most 0.00055.
The roundings to bfloat16 on the way count: a program that leaves them out, or rounds other values in their place, can miss the bound.
Values may be sent and summed in bfloat16 or wider, within the bound.
No kernel may reach another device: no remote copies, remote signals or barrier semaphores. Data moves between devices by JAX's collectives and lax.ppermute only.
A program may use at most 128 MiB of HBM per device.

v0:
```python
import jax
import jax.numpy as jnp
from jax import lax
from jax.sharding import PartitionSpec as P

ITERS = 3
teacher_temp = 0.07
student_temp = 0.1
epsilon = 1e-06


def unit(matrix):
    values = matrix.astype(jnp.float32)
    factor = lax.rsqrt(jnp.sum(values * values, axis=0, keepdims=True) + epsilon)
    return ((values * factor).astype(jnp.bfloat16), factor)


def cosine(left, right):
    return lax.dot_general(
        left, right, (((0,), (0,)), ((), ())), preferred_element_type=jnp.float32
    )


def shards(teacher_emb, student_emb, prototypes):
    teacher_full, student_full = (
        lax.all_gather(teacher_emb, "proto", axis=0, tiled=True),
        lax.all_gather(student_emb, "proto", axis=0, tiled=True),
    )
    proto_full = lax.all_gather(prototypes, "batch", axis=0, tiled=True)
    proto_unit, proto_scale = unit(proto_full)
    teacher_unit, unused = unit(teacher_full)
    student_unit, student_scale = unit(student_full)
    width = proto_full.shape[0]
    local_rows = teacher_full.shape[1]
    total_rows = local_rows * lax.axis_size("batch")
    expo = jnp.exp(cosine(teacher_unit, proto_unit) / teacher_temp)
    targets = expo
    for iteration in range(ITERS):
        column_total = lax.psum(jnp.sum(targets, axis=0), "batch")
        targets = targets / column_total[None, :]
        row_total = lax.psum(jnp.sum(targets, axis=1), "proto")
        targets = targets / row_total[:, None]
    cos_student = cosine(student_unit, proto_unit)
    logits = cos_student / student_temp
    partial_total = jnp.sum(jnp.exp(logits), axis=1)
    softmax_total = lax.psum(partial_total, "proto")
    logp = logits - jnp.log(softmax_total)[:, None]
    loss_part = -jnp.sum(targets * logp)
    loss = lax.psum(loss_part, ("batch", "proto")) / total_rows
    grad_logit = ((jnp.exp(logp) - targets) / (total_rows * student_temp)).astype(jnp.bfloat16)
    proto_rows = width // lax.axis_size("batch")
    crop_rows = width // lax.axis_size("proto")
    proto_start = lax.axis_index("batch") * proto_rows
    crop_start = lax.axis_index("proto") * crop_rows
    proto_own = lax.dynamic_slice_in_dim(proto_unit, proto_start, proto_rows, 0).astype(jnp.float32)
    student_own = lax.dynamic_slice_in_dim(student_unit, crop_start, crop_rows, 0).astype(
        jnp.float32
    )
    rows = student_unit
    proto_part = lax.psum_scatter(
        jnp.dot(rows, grad_logit, preferred_element_type=jnp.float32),
        "batch",
        scatter_dimension=0,
        tiled=True,
    )
    rows = proto_unit
    crop_part = lax.psum_scatter(
        lax.dot_general(
            rows, grad_logit, (((1,), (1,)), ((), ())), preferred_element_type=jnp.float32
        ),
        "proto",
        scatter_dimension=0,
        tiled=True,
    )
    proto_dot = lax.psum(jnp.sum(proto_own * proto_part, axis=0), "batch")
    crop_dot = lax.psum(jnp.sum(student_own * crop_part, axis=0), "proto")
    grad_proto = (proto_part - proto_own * proto_dot[None, :]) * proto_scale
    grad_student = (crop_part - student_own * crop_dot[None, :]) * student_scale
    return (grad_proto, grad_student, loss)


def solution(mesh):
    in_specs = (P("proto", "batch"), P("proto", "batch"), P("batch", "proto"))
    out_specs = (P("batch", "proto"), P("proto", "batch"), P())
    return jax.shard_map(shards, mesh=mesh, in_specs=in_specs, out_specs=out_specs, check_vma=False)
```

profile of v0, /device:TPU:0, one launch (start us, length us, event | category | flops | bytes accessed | tf_op | source)
XLA Modules:
  0.0 381.8 jit_solution(16406410473220215280)
XLA Ops:
  7.9 16.1 %all_gather.11 = bf16[256,512]{1,0:T(8,128)(2,1)S(1)} all-gather(bf16[32,512]{1,0:T(8,128)(2,1)} %param.3), channel_id=1, replica_groups=mesh['batch'=4,'proto'=8] {'proto'}, dimensions={0}, use_global_device_ids=true | all-gather | bytes 294912 | tf_op jit(solution)/shard_map/all_gather | solution.py:26
  24.1 14.4 %all_gather.9 = bf16[256,512]{1,0:T(8,128)(2,1)S(1)} all-gather(bf16[32,512]{1,0:T(8,128)(2,1)} %param.4), channel_id=1, replica_groups=mesh['batch'=4,'proto'=8] {'proto'}, dimensions={0}, use_global_device_ids=true | all-gather | bytes 294912 | tf_op jit(solution)/shard_map/all_gather | solution.py:27
  38.7 26.5 %all-gather.2.cloned.1.call-done = bf16[256,8192]{1,0:T(8,128)(2,1)} async-done(((bf16[64,8192]{1,0:T(8,128)(2,1)}), bf16[256,8192]{1,0:T(8,128)(2,1)}) %all-gather.2.cloned.1.call-update) | async-done | bytes 4194320 | tf_op jit(solution)/shard_map/all_gather | solution.py:29
  68.2 3.3 fusion.12
  73.6 7.2 %fusion.25 = (f32[8192]{0:T(1024)S(1)}, f32[512,8192]{1,0:T(8,128)}) fusion(bf16[256,8192]{1,0:T(8,128)(2,1)S(1)} %fusion.12, bf16[256,512]{1,0:T(8,128)(2,1)S(1)} %all_gather.11, f32[512]{0:T(512)S(1)} %add_rsqrt_fusion.1), kind=kOutput, calls=%fused_computation.44 | convolution fusion | flops 2156257280 | bytes 21268480 | tf_op jit(solution)/shard_map/dot_general | solution.py:19
  80.9 15.4 %psum.71 = f32[8192]{0:T(1024)S(1)} all-reduce(f32[8192]{0:T(1024)S(1)} %get-tuple-element.9), channel_id=1, replica_groups=mesh['batch'=4,'proto'=8] {'batch'}, use_global_device_ids=true, to_apply=%region_6.0 | all-reduce | flops 8192 | bytes 65536 | tf_op jit(solution)/shard_map/psum | solution.py:39
  96.3 7.0 %divide_reduce_fusion = f32[512]{0:T(512)S(1)} fusion(f32[512,8192]{1,0:T(8,128)} %get-tuple-element.10, f32[8192]{0:T(1024)S(1)} %psum.71), kind=kLoop, calls=%fused_computation.13 | loop fusion | flops 8388096 | bytes 16812032 | tf_op jit(solution)/shard_map/reduce_sum | solution.py:41
  103.3 13.6 %psum.72 = f32[512]{0:T(512)S(1)} all-reduce(f32[512]{0:T(512)S(1)} %divide_reduce_fusion), channel_id=1, replica_groups=mesh['batch'=4,'proto'=8] {'proto'}, use_global_device_ids=true, to_apply=%region_8.0 | all-reduce | flops 512 | bytes 4096 | tf_op jit(solution)/shard_map/psum | solution.py:41
  116.9 8.4 %fusion.7 = f32[8192]{0:T(1024)S(1)} fusion(f32[512,8192]{1,0:T(8,128)} %get-tuple-element.10, f32[512]{0:T(512)S(1)} %psum.72, f32[8192]{0:T(1024)S(1)} %psum.71), kind=kLoop, calls=%fused_computation.14 | loop fusion | flops 12574720 | bytes 16844800 | tf_op jit(solution)/shard_map/reduce_sum | solution.py:39
  125.3 15.1 %psum.73 = f32[8192]{0:T(1024)S(1)} all-reduce(f32[8192]{0:T(1024)S(1)} %fusion.7), channel_id=1, replica_groups=mesh['batch'=4,'proto'=8] {'batch'}, use_global_device_ids=true, to_apply=%region_10.0 | all-reduce | flops 8192 | bytes 65536 | tf_op jit(solution)/shard_map/psum | solution.py:39
  140.4 8.7 %fusion.8 = f32[512]{0:T(512)S(1)} fusion(f32[512,8192]{1,0:T(8,128)} %get-tuple-element.10, f32[8192]{0:T(1024)S(1)} %psum.73, f32[512]{0:T(512)S(1)} %psum.72, f32[8192]{0:T(1024)S(1)} %psum.71), kind=kLoop, calls=%fused_computation.15 | loop fusion | flops 16776704 | bytes 16846848 | tf_op jit(solution)/shard_map/reduce_sum | solution.py:41
  149.1 13.6 %psum.74 = f32[512]{0:T(512)S(1)} all-reduce(f32[512]{0:T(512)S(1)} %fusion.8), channel_id=1, replica_groups=mesh['batch'=4,'proto'=8] {'proto'}, use_global_device_ids=true, to_apply=%region_12.0 | all-reduce | flops 512 | bytes 4096 | tf_op jit(solution)/shard_map/psum | solution.py:41
  162.7 7.8 %fusion.9 = f32[8192]{0:T(1024)S(1)} fusion(f32[512,8192]{1,0:T(8,128)} %get-tuple-element.10, f32[512]{0:T(512)S(1)} %psum.74, f32[8192]{0:T(1024)S(1)} %psum.73, f32[512]{0:T(512)S(1)} %psum.72, f32[8192]{0:T(1024)S(1)} %psum.71), kind=kLoop, calls=%fused_computation.16 | loop fusion | flops 20963328 | bytes 16879616 | tf_op jit(solution)/shard_map/reduce_sum | solution.py:39
  170.5 15.3 %psum.75 = f32[8192]{0:T(1024)S(1)} all-reduce(f32[8192]{0:T(1024)S(1)} %fusion.9), channel_id=1, replica_groups=mesh['batch'=4,'proto'=8] {'batch'}, use_global_device_ids=true, to_apply=%region_14.0 | all-reduce | flops 8192 | bytes 65536 | tf_op jit(solution)/shard_map/psum | solution.py:39
  185.9 8.4 %fusion.10 = f32[512]{0:T(512)S(1)} fusion(f32[512,8192]{1,0:T(8,128)} %get-tuple-element.10, f32[8192]{0:T(1024)S(1)} %psum.75, f32[512]{0:T(512)S(1)} %psum.74, f32[8192]{0:T(1024)S(1)} %psum.73, f32[512]{0:T(512)S(1)} %psum.72, f32[8192]{0:T(1024)S(1)} %psum.71), kind=kLoop, calls=%fused_computation.17 | loop fusion | flops 25165312 | bytes 16881664 | tf_op jit(solution)/shard_map/reduce_sum | solution.py:41
  194.3 7.2 %exponential_reduce_fusion = (f32[512]{0:T(512)S(1)}, f32[512,8192]{1,0:T(8,128)}) fusion(bf16[256,512]{1,0:T(8,128)(2,1)S(1)} %fusion.17, bf16[256,8192]{1,0:T(8,128)(2,1)S(1)} %copy-done.1), kind=kOutput, calls=%fused_computation.12 | convolution fusion | flops 2155871744 | bytes 21235712 | tf_op jit(solution)/shard_map/dot_general | solution.py:19
  201.5 13.8 %all-reduce = (f32[512]{0:T(512)S(1)}, f32[512]{0:T(512)S(1)}) all-reduce(f32[512]{0:T(512)S(1)} %get-tuple-element.7, f32[512]{0:T(512)S(1)} %fusion.10), channel_id=1, replica_groups=mesh['batch'=4,'proto'=8] {'proto'}, use_global_device_ids=true, to_apply=%region_3.0 | all-reduce | flops 1024 | bytes 8192 | tf_op jit(solution)/shard_map/psum | solution.py:46
  215.3 15.3 %multiply_reduce_fusion = (f32[]{:T(128)}, bf16[512,8192]{1,0:T(8,128)(2,1)S(1)}) fusion(f32[512,8192]{1,0:T(8,128)} %get-tuple-element.8, f32[512]{0:T(512)S(1)} %log.3, f32[512,8192]{1,0:T(8,128)} %get-tuple-element.10, f32[512]{0:T(512)S(1)} %get-tuple-element.4, f32[8192]{0:T(1024)S(1)} %psum.75, f32[512]{0:T(512)S(1)} %psum.74, f32[8192]{0:T(1024)S(1)} %psum.73, ...), kind=kLoop, calls=%fused_computation.9 | loop fusion | flops 54525952 | bytes 42049540 | tf_op jit(solution)/shard_map/reduce_sum | solution.py:48
  237.0 9.0 %fusion.26 = f32[256,8192]{1,0:T(8,128)} fusion(bf16[256,512]{1,0:T(8,128)(2,1)S(1)} %fusion.17, bf16[512,8192]{1,0:T(8,128)(2,1)} %copy-done.3), kind=kOutput, calls=%fused_computation.45 | convolution fusion | flops 2147483648 | bytes 17039360 | tf_op jit(solution)/shard_map/dot_general | solution.py:61
  246.7 37.5 %psum.79 = f32[]{:T(128)} all-reduce(f32[]{:T(128)S(6)} %neg.3), channel_id=1, replica_groups=mesh['batch'=4,'proto'=8] {'batch','proto'}, use_global_device_ids=true, to_apply=%region_24.0 | all-reduce | flops 1 | bytes 8 | tf_op jit(solution)/shard_map/psum | solution.py:49
  285.8 15.5 %psum.78 = f32[512]{0:T(512)S(1)} all-reduce(f32[512]{0:T(512)S(1)} %fusion.22), channel_id=1, replica_groups=mesh['batch'=4,'proto'=8] {'proto'}, use_global_device_ids=true, to_apply=%region_22.0 | all-reduce | flops 512 | bytes 4096 | tf_op jit(solution)/shard_map/psum | solution.py:76
  302.7 50.4 %reduce-scatter.3.cloned.1.call-done = f32[64,8192]{1,0:T(8,128)} async-done(((f32[256,8192]{1,0:T(8,128)}), f32[64,8192]{1,0:T(8,128)}) %reduce-scatter.3.cloned.1.call-update) | async-done | bytes 2097168 | tf_op jit(solution)/shard_map/reduce_scatter | solution.py:60
  355.2 15.4 %psum.77 = f32[8192]{0:T(1024)S(1)} all-reduce(f32[8192]{0:T(1024)S(1)} %fusion.13), channel_id=1, replica_groups=mesh['batch'=4,'proto'=8] {'batch'}, use_global_device_ids=true, to_apply=%region_19.0 | all-reduce | flops 8192 | bytes 65536 | tf_op jit(solution)/shard_map/psum | solution.py:75
  370.6 3.5 fusion.15
  (27 shorter events, 17.1 us)
Async XLA Ops:
  7.2 58.0 %all-gather.2.cloned.1.call-start = ((), (), s32[]{:S(2)}) async-start(), calls=%async_computation.2 | async-start | bytes 5242880 | tf_op jit(solution)/shard_map/all_gather | solution.py:29
  7.9 277.0 %reduce-scatter.5.cloned.1.call-start = ((), (), s32[]{:S(2)}) async-start(), calls=%async_computation.4 | async-start | bytes 589824 | tf_op jit(solution)/shard_map/reduce_scatter | solution.py:67
  71.6 2.0 copy-start
  185.8 8.4 %copy-start.1 = (bf16[256,8192]{1,0:T(8,128)(2,1)S(1)}, bf16[256,8192]{1,0:T(8,128)(2,1)}, u32[]{:S(2)}) copy-start(bf16[256,8192]{1,0:T(8,128)(2,1)} %copy-done) | copy-start | bytes 12582916
  215.3 18.5 %copy-start.2 = (bf16[256,8192]{1,0:T(8,128)(2,1)S(1)}, bf16[256,8192]{1,0:T(8,128)(2,1)}, u32[]{:S(2)}) copy-start(bf16[256,8192]{1,0:T(8,128)(2,1)} %copy-done) | copy-start | bytes 12582916
  230.5 3.2 copy-start.3
  236.9 116.2 %reduce-scatter.3.cloned.1.call-start = ((), (), s32[]{:S(2)}) async-start(), calls=%async_computation.3 | async-start | bytes 10485760 | tf_op jit(solution)/shard_map/reduce_scatter | solution.py:60
Sparse Core Ops, SparseCore 0:
  9.8 55.2 all-gather.1
  237.0 27.9 reduce-scatter.4
  268.1 84.9 reduce-scatter.2
where the time goes:
time: 382 us
  blocking collectives  186 us (49%)
  waiting for transfers between devices  77.5 us (20%)
  other arithmetic  70.2 us (18%)
  matrix products  26.6 us (7%)
  between operations  16.3 us (4%)
  local copies, waits for them, and re-layouts  5.26 us (1%)
    reduce_scatter x1, waiting for transfers between devices, shards(): lax.psum_scatter(jnp.dot(rows, grad_logit, preferred_element_type=jnp.flo...  50.4 us
    psum x3, blocking collectives, shards(): column_total = lax.psum(jnp.sum(targets, axis=0), 'batch')  45.8 us
    psum x1, blocking collectives, shards(): loss = lax.psum(loss_part, ('batch', 'proto')) / total_rows  37.5 us
    psum x2, blocking collectives, shards(): row_total = lax.psum(jnp.sum(targets, axis=1), 'proto')  27.2 us
    all_gather x1, waiting for transfers between devices, shards(): proto_full = lax.all_gather(prototypes, 'batch', axis=0, tiled=True)  26.5 us
    reduce_sum x3, other arithmetic, shards(): row_total = lax.psum(jnp.sum(targets, axis=1), 'proto')  24.2 us
    reduce_sum x2, other arithmetic, shards(): column_total = lax.psum(jnp.sum(targets, axis=0), 'batch')  16.2 us
    all_gather x1, blocking collectives, shards(): lax.all_gather(teacher_emb, 'proto', axis=0, tiled=True)  16.1 us
  transfers between devices with their start and end apart: 3, of which 2 were waited for; matrix products, arithmetic and copies ran while one was open for 3% of the time, Pallas kernels for 0%

commit v1 on v0

--- a/solution.py
+++ b/solution.py
@@ -26,7 +26,21 @@
         lax.all_gather(teacher_emb, "proto", axis=0, tiled=True),
         lax.all_gather(student_emb, "proto", axis=0, tiled=True),
     )
-    proto_full = lax.all_gather(prototypes, "batch", axis=0, tiled=True)
+    trail = [prototypes]
+    n_peers_all = lax.axis_size("batch")
+    for hop_no in tuple(range(n_peers_all - 1)):
+        trail.append(
+            lax.ppermute(
+                trail[-1],
+                axis_name="batch",
+                perm=[(c, (c + 1) % n_peers_all) for c in range(n_peers_all)],
+            )
+        )
+    proto_full = jnp.roll(
+        jnp.concatenate(trail[::-1], axis=0),
+        shift=(lax.axis_index("batch") + 1) * prototypes.shape[0],
+        axis=0,
+    )
     proto_unit, proto_scale = unit(proto_full)
     teacher_unit, unused = unit(teacher_full)
     student_unit, student_scale = unit(student_full)

time: 382 us -> 399 us (1.045)
  waiting for transfers between devices: 77.5 us -> 95 us
  other arithmetic: 70.2 us -> 65.6 us
    ppermute x0 -> x3, waiting for transfers between devices: none -> 43.7 us  [shards(): lax.ppermute(trail[-1], axis_name='batch', perm=[(c, (c + 1) % n_peers_al...]
    all_gather x1 -> x0, waiting for transfers between devices: 26.5 us -> none  [shards(): proto_full = lax.all_gather(prototypes, 'batch', axis=0, tiled=True)]
  transfers between devices with their start and end apart: 3 -> 5, of which waited for: 2 -> 4; matrix products, arithmetic and copies ran while one was open for 3% -> 3% of each run, Pallas kernels for 0% -> 0%
where the time goes in v1:
time: 399 us; the launch traced here: 398 us
  blocking collectives  183 us (46%)
  waiting for transfers between devices  95 us (24%)
  other arithmetic  65.6 us (16%)
  matrix products  26.5 us (7%)
  between operations  16.7 us (4%)
  local copies, waits for them, and re-layouts  7.06 us (2%)
    reduce_scatter x1, waiting for transfers between devices, shards(): lax.psum_scatter(jnp.dot(rows, grad_logit, preferred_element_type=jnp.flo...  51.2 us
    psum x3, blocking collectives, shards(): column_total = lax.psum(jnp.sum(targets, axis=0), 'batch')  44.2 us
    ppermute x3, waiting for transfers between devices, shards(): lax.ppermute(trail[-1], axis_name='batch', perm=[(c, (c + 1) % n_peers_al...  43.7 us
    psum x1, blocking collectives, shards(): loss = lax.psum(loss_part, ('batch', 'proto')) / total_rows  38 us
    psum x2, blocking collectives, shards(): row_total = lax.psum(jnp.sum(targets, axis=1), 'proto')  27.2 us
    reduce_sum x3, other arithmetic, shards(): row_total = lax.psum(jnp.sum(targets, axis=1), 'proto')  24.2 us
    reduce_sum x2, other arithmetic, shards(): column_total = lax.psum(jnp.sum(targets, axis=0), 'batch')  16.2 us
    psum x1, blocking collectives, shards(): crop_dot = lax.psum(jnp.sum(student_own * crop_part, axis=0), 'proto')  15.5 us
  transfers between devices with their start and end apart: 5, of which 4 were waited for; matrix products, arithmetic and copies ran while one was open for 3% of the time, Pallas kernels for 0%

profile of v1, /device:TPU:0, one launch (start us, length us, event | category | flops | bytes accessed | tf_op | source)
XLA Modules:
  0.0 398.0 jit_solution(7545715562320464752)
XLA Ops:
  10.2 24.3 %collective-permute-done = bf16[64,8192]{1,0:T(8,128)(2,1)S(1)} collective-permute-done((bf16[64,8192]{1,0:T(8,128)(2,1)}, bf16[64,8192]{1,0:T(8,128)(2,1)S(1)}, u32[]{:S(2)}, u32[]{:S(2)}) %collective-permute-start) | collective-permute-done | bytes 1048608 | tf_op jit(solution)/shard_map/ppermute | solution.py:33
  35.4 14.6 %all_gather.7 = bf16[256,512]{1,0:T(8,128)(2,1)S(1)} all-gather(bf16[32,512]{1,0:T(8,128)(2,1)} %param.3), channel_id=1, replica_groups=mesh['batch'=4,'proto'=8] {'proto'}, dimensions={0}, use_global_device_ids=true | all-gather | bytes 294912 | tf_op jit(solution)/shard_map/all_gather | solution.py:26
  50.0 9.8 %collective-permute-done.1 = bf16[64,8192]{1,0:T(8,128)(2,1)S(1)} collective-permute-done((bf16[64,8192]{1,0:T(8,128)(2,1)S(1)}, bf16[64,8192]{1,0:T(8,128)(2,1)S(1)}, u32[]{:S(2)}, u32[]{:S(2)}) %collective-permute-start.1) | collective-permute-done | bytes 1048608 | tf_op jit(solution)/shard_map/ppermute | solution.py:33
  59.8 14.5 %all_gather.6 = bf16[256,512]{1,0:T(8,128)(2,1)S(1)} all-gather(bf16[32,512]{1,0:T(8,128)(2,1)} %param.4), channel_id=1, replica_groups=mesh['batch'=4,'proto'=8] {'proto'}, dimensions={0}, use_global_device_ids=true | all-gather | bytes 294912 | tf_op jit(solution)/shard_map/all_gather | solution.py:27
  74.6 9.6 %collective-permute-done.2 = bf16[64,8192]{1,0:T(8,128)(2,1)S(1)} collective-permute-done((bf16[64,8192]{1,0:T(8,128)(2,1)S(1)}, bf16[64,8192]{1,0:T(8,128)(2,1)S(1)}, u32[]{:S(2)}, u32[]{:S(2)}) %collective-permute-start.2) | collective-permute-done | bytes 1048608 | tf_op jit(solution)/shard_map/ppermute | solution.py:33
  89.9 7.2 %fusion.25 = (f32[8192]{0:T(1024)S(1)}, f32[512,8192]{1,0:T(8,128)}) fusion(bf16[256,8192]{1,0:T(8,128)(2,1)S(1)} %fusion.12, bf16[256,512]{1,0:T(8,128)(2,1)S(1)} %all_gather.7, f32[512]{0:T(512)S(1)} %add_rsqrt_fusion.1), kind=kOutput, calls=%fused_computation.52 | convolution fusion | flops 2156257280 | bytes 21268480 | tf_op jit(solution)/shard_map/dot_general | solution.py:19
  97.1 14.0 %psum.71 = f32[8192]{0:T(1024)S(1)} all-reduce(f32[8192]{0:T(1024)S(1)} %get-tuple-element.9), channel_id=1, replica_groups=mesh['batch'=4,'proto'=8] {'batch'}, use_global_device_ids=true, to_apply=%region_6.7 | all-reduce | flops 8192 | bytes 65536 | tf_op jit(solution)/shard_map/psum | solution.py:53
  111.1 7.0 %divide_reduce_fusion = f32[512]{0:T(512)S(1)} fusion(f32[512,8192]{1,0:T(8,128)} %get-tuple-element.10, f32[8192]{0:T(1024)S(1)} %psum.71), kind=kLoop, calls=%fused_computation.13 | loop fusion | flops 8388096 | bytes 16812032 | tf_op jit(solution)/shard_map/reduce_sum | solution.py:55
  118.1 13.6 %psum.72 = f32[512]{0:T(512)S(1)} all-reduce(f32[512]{0:T(512)S(1)} %divide_reduce_fusion), channel_id=1, replica_groups=mesh['batch'=4,'proto'=8] {'proto'}, use_global_device_ids=true, to_apply=%region_8.9 | all-reduce | flops 512 | bytes 4096 | tf_op jit(solution)/shard_map/psum | solution.py:55
  131.7 8.4 %fusion.7 = f32[8192]{0:T(1024)S(1)} fusion(f32[512,8192]{1,0:T(8,128)} %get-tuple-element.10, f32[512]{0:T(512)S(1)} %psum.72, f32[8192]{0:T(1024)S(1)} %psum.71), kind=kLoop, calls=%fused_computation.14 | loop fusion | flops 12574720 | bytes 16844800 | tf_op jit(solution)/shard_map/reduce_sum | solution.py:53
  140.1 16.2 %psum.73 = f32[8192]{0:T(1024)S(1)} all-reduce(f32[8192]{0:T(1024)S(1)} %fusion.7), channel_id=1, replica_groups=mesh['batch'=4,'proto'=8] {'batch'}, use_global_device_ids=true, to_apply=%region_10.11 | all-reduce | flops 8192 | bytes 65536 | tf_op jit(solution)/shard_map/psum | solution.py:53
  156.3 8.7 %fusion.8 = f32[512]{0:T(512)S(1)} fusion(f32[512,8192]{1,0:T(8,128)} %get-tuple-element.10, f32[8192]{0:T(1024)S(1)} %psum.73, f32[512]{0:T(512)S(1)} %psum.72, f32[8192]{0:T(1024)S(1)} %psum.71), kind=kLoop, calls=%fused_computation.15 | loop fusion | flops 16776704 | bytes 16846848 | tf_op jit(solution)/shard_map/reduce_sum | solution.py:55
  165.1 13.6 %psum.74 = f32[512]{0:T(512)S(1)} all-reduce(f32[512]{0:T(512)S(1)} %fusion.8), channel_id=1, replica_groups=mesh['batch'=4,'proto'=8] {'proto'}, use_global_device_ids=true, to_apply=%region_12.13 | all-reduce | flops 512 | bytes 4096 | tf_op jit(solution)/shard_map/psum | solution.py:55
  178.6 7.8 %fusion.9 = f32[8192]{0:T(1024)S(1)} fusion(f32[512,8192]{1,0:T(8,128)} %get-tuple-element.10, f32[512]{0:T(512)S(1)} %psum.74, f32[8192]{0:T(1024)S(1)} %psum.73, f32[512]{0:T(512)S(1)} %psum.72, f32[8192]{0:T(1024)S(1)} %psum.71), kind=kLoop, calls=%fused_computation.16 | loop fusion | flops 20963328 | bytes 16879616 | tf_op jit(solution)/shard_map/reduce_sum | solution.py:53
  186.4 14.1 %psum.75 = f32[8192]{0:T(1024)S(1)} all-reduce(f32[8192]{0:T(1024)S(1)} %fusion.9), channel_id=1, replica_groups=mesh['batch'=4,'proto'=8] {'batch'}, use_global_device_ids=true, to_apply=%region_14.15 | all-reduce | flops 8192 | bytes 65536 | tf_op jit(solution)/shard_map/psum | solution.py:53
  200.5 8.4 %fusion.10 = f32[512]{0:T(512)S(1)} fusion(f32[512,8192]{1,0:T(8,128)} %get-tuple-element.10, f32[8192]{0:T(1024)S(1)} %psum.75, f32[512]{0:T(512)S(1)} %psum.74, f32[8192]{0:T(1024)S(1)} %psum.73, f32[512]{0:T(512)S(1)} %psum.72, f32[8192]{0:T(1024)S(1)} %psum.71), kind=kLoop, calls=%fused_computation.17 | loop fusion | flops 25165312 | bytes 16881664 | tf_op jit(solution)/shard_map/reduce_sum | solution.py:55
  209.0 7.2 %exponential_reduce_fusion = (f32[512]{0:T(512)S(1)}, f32[512,8192]{1,0:T(8,128)}) fusion(bf16[256,512]{1,0:T(8,128)(2,1)S(1)} %fusion.17, bf16[256,8192]{1,0:T(8,128)(2,1)S(1)} %copy-done.1), kind=kOutput, calls=%fused_computation.12 | convolution fusion | flops 2155871744 | bytes 21235712 | tf_op jit(solution)/shard_map/dot_general | solution.py:19
  216.1 13.8 %all-reduce = (f32[512]{0:T(512)S(1)}, f32[512]{0:T(512)S(1)}) all-reduce(f32[512]{0:T(512)S(1)} %get-tuple-element.7, f32[512]{0:T(512)S(1)} %fusion.10), channel_id=1, replica_groups=mesh['batch'=4,'proto'=8] {'proto'}, use_global_device_ids=true, to_apply=%region_3.4 | all-reduce | flops 1024 | bytes 8192 | tf_op jit(solution)/shard_map/psum | solution.py:60
  229.9 15.3 %multiply_reduce_fusion = (f32[]{:T(128)}, bf16[512,8192]{1,0:T(8,128)(2,1)S(1)}) fusion(f32[512,8192]{1,0:T(8,128)} %get-tuple-element.8, f32[512]{0:T(512)S(1)} %log.3, f32[512,8192]{1,0:T(8,128)} %get-tuple-element.10, f32[512]{0:T(512)S(1)} %get-tuple-element.4, f32[8192]{0:T(1024)S(1)} %psum.75, f32[512]{0:T(512)S(1)} %psum.74, f32[8192]{0:T(1024)S(1)} %psum.73, ...), kind=kLoop, calls=%fused_computation.9 | loop fusion | flops 54525952 | bytes 42049540 | tf_op jit(solution)/shard_map/reduce_sum | solution.py:62
  251.6 9.0 %fusion.26 = f32[256,8192]{1,0:T(8,128)} fusion(bf16[256,512]{1,0:T(8,128)(2,1)S(1)} %fusion.17, bf16[512,8192]{1,0:T(8,128)(2,1)} %copy-done.3), kind=kOutput, calls=%fused_computation.53 | convolution fusion | flops 2147483648 | bytes 17039360 | tf_op jit(solution)/shard_map/dot_general | solution.py:75
  261.3 38.0 %psum.79 = f32[]{:T(128)} all-reduce(f32[]{:T(128)S(6)} %neg.3), channel_id=1, replica_groups=mesh['batch'=4,'proto'=8] {'batch','proto'}, use_global_device_ids=true, to_apply=%region_24.25 | all-reduce | flops 1 | bytes 8 | tf_op jit(solution)/shard_map/psum | solution.py:63
  300.8 15.5 %psum.78 = f32[512]{0:T(512)S(1)} all-reduce(f32[512]{0:T(512)S(1)} %fusion.22), channel_id=1, replica_groups=mesh['batch'=4,'proto'=8] {'proto'}, use_global_device_ids=true, to_apply=%region_22.23 | all-reduce | flops 512 | bytes 4096 | tf_op jit(solution)/shard_map/psum | solution.py:90
  317.8 51.2 %reduce-scatter.3.cloned.1.call-done = f32[64,8192]{1,0:T(8,128)} async-done(((f32[256,8192]{1,0:T(8,128)}), f32[64,8192]{1,0:T(8,128)}) %reduce-scatter.3.cloned.1.call-update) | async-done | bytes 2097168 | tf_op jit(solution)/shard_map/reduce_scatter | solution.py:74
  371.1 15.4 %psum.77 = f32[8192]{0:T(1024)S(1)} all-reduce(f32[8192]{0:T(1024)S(1)} %fusion.13), channel_id=1, replica_groups=mesh['batch'=4,'proto'=8] {'batch'}, use_global_device_ids=true, to_apply=%region_19.20 | all-reduce | flops 8192 | bytes 65536 | tf_op jit(solution)/shard_map/psum | solution.py:89
  (40 shorter events, 24.1 us)
Async XLA Ops:
  7.2 78.8 %copy-start.4 = (bf16[64,8192]{1,0:T(8,128)(2,1)S(1)}, bf16[64,8192]{1,0:T(8,128)(2,1)}, u32[]{:S(2)}) copy-start(bf16[64,8192]{1,0:T(8,128)(2,1)} %param.5) | copy-start | bytes 3145732
  7.2 292.7 %reduce-scatter.5.cloned.1.call-start = ((), (), s32[]{:S(2)}) async-start(), calls=%async_computation.3 | async-start | bytes 589824 | tf_op jit(solution)/shard_map/reduce_scatter | solution.py:81
  7.2 27.3 %collective-permute-start = (bf16[64,8192]{1,0:T(8,128)(2,1)}, bf16[64,8192]{1,0:T(8,128)(2,1)S(1)}, u32[]{:S(2)}, u32[]{:S(2)}) collective-permute-start(bf16[64,8192]{1,0:T(8,128)(2,1)} %param.5), channel_id=1, source_target_pairs={{0,8},{8,16},{16,24},{24,0},{1,9},{9,17},{17,25},{25,1},{2,10},{10... | collective-permute-start | bytes 3145736 | tf_op jit(solution)/shard_map/ppermute | solution.py:33
  34.6 25.2 %collective-permute-start.1 = (bf16[64,8192]{1,0:T(8,128)(2,1)S(1)}, bf16[64,8192]{1,0:T(8,128)(2,1)S(1)}, u32[]{:S(2)}, u32[]{:S(2)}) collective-permute-start(bf16[64,8192]{1,0:T(8,128)(2,1)S(1)} %collective-permute-done), channel_id=1, source_target_pairs={{0,8},{8,16},{16,24},{24,0},{1,9},{9,17},{17,25},{25,1},{2,10},{10... | collective-permute-start | bytes 3145736 | tf_op jit(solution)/shard_map/ppermute | solution.py:33
  59.8 24.4 %collective-permute-start.2 = (bf16[64,8192]{1,0:T(8,128)(2,1)S(1)}, bf16[64,8192]{1,0:T(8,128)(2,1)S(1)}, u32[]{:S(2)}, u32[]{:S(2)}) collective-permute-start(bf16[64,8192]{1,0:T(8,128)(2,1)S(1)} %collective-permute-done.1), channel_id=1, source_target_pairs={{0,8},{8,16},{16,24},{24,0},{1,9},{9,17},{17,25},{25,1},{2,10},{10... | collective-permute-start | bytes 3145736 | tf_op jit(solution)/shard_map/ppermute | solution.py:33
  87.8 2.0 copy-start
  200.5 8.4 %copy-start.1 = (bf16[256,8192]{1,0:T(8,128)(2,1)S(1)}, bf16[256,8192]{1,0:T(8,128)(2,1)}, u32[]{:S(2)}) copy-start(bf16[256,8192]{1,0:T(8,128)(2,1)} %copy-done) | copy-start | bytes 12582916
  229.9 18.5 %copy-start.2 = (bf16[256,8192]{1,0:T(8,128)(2,1)S(1)}, bf16[256,8192]{1,0:T(8,128)(2,1)}, u32[]{:S(2)}) copy-start(bf16[256,8192]{1,0:T(8,128)(2,1)} %copy-done) | copy-start | bytes 12582916
  245.2 3.2 copy-start.3
  251.6 117.4 %reduce-scatter.3.cloned.1.call-start = ((), (), s32[]{:S(2)}) async-start(), calls=%async_computation.2 | async-start | bytes 10485760 | tf_op jit(solution)/shard_map/reduce_scatter | solution.py:74
Sparse Core Ops, SparseCore 0:
  251.7 28.9 reduce-scatter.4
  283.8 85.2 reduce-scatter.2
